TPU v7x, 128 devices: a whole 4x4x4 slice. The times are simulated.
128 devices in a mesh: ctx: 16 (over z_hi, x, core), head: 8 (over z_lo, y).
Axes of the slice: x: 4, y: 4, z: 4 (z_hi: 2, z_lo: 2; z = z_hi * 2 + z_lo), core: 2. Of those that a mesh axis runs over, the one named last changes fastest.
Arguments:
- tokens: bfloat16 [16384, 4096], P('ctx', 'head'), may hold values from -23 to 23
- proj_weight: bfloat16 [4096, 32, 384], P(None, 'head'), may hold values from -1 to 1
- partner_shard: int32 [32, 256, 3], P('head'), may hold values from 0 to 15, all different within a row; in each aligned block of 16 rows (0 to 15, 16 to 31, ..., all dimensions but the last counted through in order) at most 6 rows name the same one
- partner_block: int32 [32, 256, 3], P('head'), may hold values from 0 to 15
Outputs:
- attended: bfloat16 [16384, 32, 128], P('ctx', 'head')
Inputs may be any that keep to these rules, and one draw needn't show every extreme that they name: `partner_shard`: the 3 entries of one row differ. For each head, within each aligned run of 16 block rows, no value is named more than 6 times, and some runs name one value exactly 6 times.
All inputs are finite; a program needn't handle non-finite values.
Results may differ from a plain program's by a relative error of at most 0.008.
Values may be sent and summed in bfloat16 or wider, within the bound.
A program may use at most 192 MiB of HBM per device.

v0:
```python
import jax
import jax.numpy as jnp
from jax import lax
from jax.sharding import PartitionSpec as P

HEAD_DIMENSION = 128
BLK = 64
GLOB = 2
RAND = 3


def padded_2(cells, sides, width):
    for axis, dim in sides:
        count = lax.axis_size(axis)
        head = lax.slice_in_dim(cells, 0, width, axis=dim)
        tail = lax.slice_in_dim(cells, cells.shape[dim] - width, cells.shape[dim], axis=dim)
        cells = jnp.concatenate(
            [
                lax.ppermute(tail, axis, [(i, (i + 1) % count) for i in range(count)]),
                cells,
                lax.ppermute(head, axis, [((i + 1) % count, i) for i in range(count)]),
            ],
            axis=dim,
        )
    return cells


def from_root(block, axis, holder):
    block = jnp.where(lax.axis_index(axis) == holder, block, jnp.zeros_like(block))
    return lax.psum(block, axis)


def combined_all(part, axis, combine):
    gathered = jax.tree.map(lambda a: lax.all_gather(a, axis), part)

    def take(source):
        return jax.tree.map(lambda a: lax.dynamic_index_in_dim(a, source, 0, False), gathered)

    return lax.fori_loop(
        1, lax.axis_size(axis), lambda source, state: combine(state, take(source)), take(0)
    )


def per_device(tokens, proj_weight, partner_shard, partner_block):
    row_count = tokens.shape[0]
    head_count = proj_weight.shape[1]
    blocks = row_count // BLK
    shard_index = lax.axis_index("ctx")
    inverse_root_scale = HEAD_DIMENSION ** (-0.5)
    packed = jnp.einsum(
        "td,dhe->the",
        lax.all_gather(tokens, "head", axis=1, tiled=True),
        proj_weight,
        preferred_element_type=jnp.float32,
    ).astype(jnp.bfloat16)
    queries = packed[..., :HEAD_DIMENSION]
    keyval = packed[..., HEAD_DIMENSION:]
    padded = padded_2(keyval, (("ctx", 0),), BLK)
    window = jnp.concatenate(
        [
            padded[0:row_count].reshape(blocks, BLK, head_count, 2 * HEAD_DIMENSION),
            padded[BLK : row_count + BLK].reshape(blocks, BLK, head_count, 2 * HEAD_DIMENSION),
            padded[2 * BLK : row_count + 2 * BLK].reshape(
                blocks, BLK, head_count, 2 * HEAD_DIMENSION
            ),
        ],
        axis=1,
    )
    global_pack = from_root(packed[: GLOB * BLK], "ctx", 0)
    global_query = global_pack[..., :HEAD_DIMENSION]
    global_keyval = global_pack[..., HEAD_DIMENSION:]
    row_total = blocks * RAND
    owners = lax.dynamic_slice_in_dim(partner_shard, shard_index * blocks, blocks, 1).reshape(
        head_count, row_total
    )
    offsets = lax.dynamic_slice_in_dim(partner_block, shard_index * blocks, blocks, 1).reshape(
        head_count, row_total
    )
    partner_index = owners * blocks + offsets
    block_rows = lax.all_gather(keyval, "ctx", axis=0, tiled=True)
    piece_blocks = block_rows.shape[0] // BLK
    piece_hot = (partner_index[..., None] == jnp.arange(piece_blocks)).astype(jnp.bfloat16)
    blocked = block_rows.reshape(piece_blocks, BLK, head_count, 2 * HEAD_DIMENSION)
    fetched = jnp.einsum(
        "hrb,bthe->hrte", piece_hot, blocked, preferred_element_type=jnp.float32
    ).astype(jnp.bfloat16)
    remote = fetched
    remote = remote.reshape(head_count, blocks, RAND * BLK, 2 * HEAD_DIMENSION)
    blocked_query_rows = queries.reshape(blocks, BLK, head_count, HEAD_DIMENSION)
    window_scores = jnp.einsum(
        "bqhd,bkhd->bhqk",
        blocked_query_rows,
        window[..., :HEAD_DIMENSION],
        preferred_element_type=jnp.float32,
    )
    global_scores = jnp.einsum(
        "bqhd,khd->bhqk",
        blocked_query_rows,
        global_keyval[..., :HEAD_DIMENSION],
        preferred_element_type=jnp.float32,
    )
    remote_scores = jnp.einsum(
        "bqhd,hbkd->bhqk",
        blocked_query_rows,
        remote[..., :HEAD_DIMENSION],
        preferred_element_type=jnp.float32,
    )
    logit_scores = (
        jnp.concatenate([window_scores, global_scores, remote_scores], axis=-1) * inverse_root_scale
    )
    softmax_weight_matrix = jax.nn.softmax(logit_scores, axis=-1).astype(jnp.bfloat16)
    width_window = 3 * BLK
    width_global = GLOB * BLK
    context = jnp.einsum(
        "bhqk,bkhd->bqhd",
        softmax_weight_matrix[..., :width_window],
        window[..., HEAD_DIMENSION:],
        preferred_element_type=jnp.float32,
    )
    context = context + jnp.einsum(
        "bhqk,khd->bqhd",
        softmax_weight_matrix[..., width_window : width_window + width_global],
        global_keyval[..., HEAD_DIMENSION:],
        preferred_element_type=jnp.float32,
    )
    context = context + jnp.einsum(
        "bhqk,hbkd->bqhd",
        softmax_weight_matrix[..., width_window + width_global :],
        remote[..., HEAD_DIMENSION:],
        preferred_element_type=jnp.float32,
    )
    sparse_attention_output = context.astype(jnp.bfloat16).reshape(
        row_count, head_count, HEAD_DIMENSION
    )
    lead_scores = (
        jnp.einsum(
            "qhd,khd->hqk",
            global_query,
            keyval[..., :HEAD_DIMENSION],
            preferred_element_type=jnp.float32,
        )
        * inverse_root_scale
    )
    maxima = jnp.max(lead_scores, axis=-1)
    exp_terms = jnp.exp(lead_scores - maxima[..., None])
    totals = jnp.sum(exp_terms, axis=-1)
    summed = jnp.einsum(
        "hqk,khd->hqd",
        exp_terms,
        keyval[..., HEAD_DIMENSION:].astype(jnp.float32),
        precision=lax.Precision.HIGHEST,
    )

    def combine(first, second):
        max_first, total_first, sum_first = first
        max_second, total_second, sum_second = second
        larger = jnp.maximum(max_first, max_second)
        factor_first = jnp.exp(max_first - larger)
        factor_second = jnp.exp(max_second - larger)
        return (
            larger,
            total_first * factor_first + total_second * factor_second,
            sum_first * factor_first[..., None] + sum_second * factor_second[..., None],
        )

    maxima, totals, summed = combined_all((maxima, totals, summed), "ctx", combine)
    global_out = jnp.transpose((summed / totals[..., None]).astype(jnp.bfloat16), (1, 0, 2))
    head_rows = jnp.where(shard_index == 0, global_out, sparse_attention_output[: GLOB * BLK])
    return jnp.concatenate([head_rows, sparse_attention_output[GLOB * BLK :]], axis=0)


def solution(mesh):
    in_specs = (
        P("ctx", "head"),
        P(None, "head", None),
        P("head", None, None),
        P("head", None, None),
    )
    out_specs = P("ctx", "head", None)
    return jax.shard_map(
        per_device, mesh=mesh, in_specs=in_specs, out_specs=out_specs, check_vma=False
    )
```

profile of v0, /device:TPU:1, one launch (start us, length us, event | category | flops | bytes accessed | tf_op | source)
XLA Modules:
  0.0 600.8 jit_solution(12266525961735290425)
XLA Ops:
  6.5 0.7 all-gather.9.cloned.1.call-update
  7.3 0.0 all-reduce.2.cloned.1.call-start
  7.3 96.7 %all-gather.9.cloned.1.call-done = bf16[1024,4096]{1,0:T(8,128)(2,1)} async-done(((bf16[1024,512]{1,0:T(8,128)(2,1)}), bf16[1024,4096]{1,0:T(8,128)(2,1)}) %all-gather.9.cloned.1.call-update) | async-done | bytes 8388624 | tf_op jit(solution)/shard_map/all_gather | solution.py:52
  104.0 18.3 %fusion.22 = bf16[1024,4,384]{2,0,1:T(8,128)(2,1)S(1)} fusion(bf16[4096,4,384]{2,1,0:T(4,128)(2,1)} %param.7, bf16[1024,4096]{1,0:T(8,128)(2,1)} %all-gather.9.cloned.1.call-done), kind=kOutput, calls=%fused_computation.29 | convolution fusion | flops 12886474752 | bytes 24117248 | tf_op jit(solution)/shard_map/td,dhe->the/dot_general | solution.py:50
  122.3 0.8 slice_select_fusion
  123.2 0.0 all-reduce.2.cloned.1.call-update
  123.2 0.0 all-gather.13.cloned.1.call-start
  123.2 138.2 %all-reduce.2.cloned.1.call-done = bf16[128,4,384]{2,0,1:T(8,128)(2,1)} async-done(((bf16[128,4,384]{2,0,1:T(8,128)(2,1)}), bf16[128,4,384]{2,0,1:T(8,128)(2,1)}) %all-reduce.2.cloned.1.call-update) | async-done | bytes 393232 | tf_op jit(solution)/shard_map/psum | solution.py:30
  261.4 1.4 multiply_reduce_fusion
  262.8 1.3 copy-done.1
  264.1 2.2 fusion.30
  266.3 0.0 all-gather.13.cloned.1.call-update
  266.3 0.0 all-gather.11.cloned.1.call-start
  266.4 1.5 slice.118
  267.9 0.0 all-gather.11.cloned.1.call-update
  267.9 1.8 fusion.56
  269.7 0.7 collective-permute-start.1
  270.4 0.8 dynamic-slice_add_fusion
  271.1 0.1 copy.40
  271.2 0.1 add.84
  271.3 1.3 slice.116
  272.6 1.4 collective-permute-done.1
  274.1 0.3 pad_maximum_fusion.2
  274.4 5.0 pad_maximum_fusion
  279.4 3.4 fusion.54
  282.8 4.1 fusion.20
  286.9 25.5 %all-gather.3 = f32[16,4,128]{2,1,0:T(4,128)S(1)} all-gather(f32[1,4,128]{2,1,0:T(4,128)S(1)} %bitcast.75), channel_id=2, replica_groups=mesh['ctx'=16,'head'=8] {'ctx'}, dimensions={0}, use_global_device_ids=true | all-gather | bytes 34816 | tf_op jit(solution)/shard_map/all_gather | solution.py:34
  312.4 0.5 fusion.31
  312.9 19.5 %all-gather.4 = f32[16,4,128]{2,1,0:T(4,128)S(1)} all-gather(f32[1,4,128]{2,1,0:T(4,128)S(1)} %bitcast.76), channel_id=3, replica_groups=mesh['ctx'=16,'head'=8] {'ctx'}, dimensions={0}, use_global_device_ids=true | all-gather | bytes 34816 | tf_op jit(solution)/shard_map/all_gather | solution.py:34
  332.4 1.3 convolution_bitcast_fusion
  333.7 0.0 all-gather.13.cloned.1.call-done
  333.8 1.0 slice.115
  334.8 19.0 %while.19 = (s32[]{:T(128)}, f32[4,128]{1,0:T(4,128)S(1)}, f32[4,128]{1,0:T(4,128)S(1)}, f32[4,128,128]{2,1,0:T(8,128)S(1)}, f32[16,4,128]{2,1,0:T(4,128)S(1)}, ...) while((s32[]{:T(128)}, f32[4,128]{1,0:T(4,128)S(1)}, ...), condition=%wide.region_4.5_spmd, body=%wide.region_3.4_spmd.sunk | while | flops 199685 | bytes 807063 | solution.py:39
  334.8 1.3 fusion.61
  336.1 1.2 fusion.61
  337.4 1.2 fusion.61
  338.7 1.3 fusion.61
  340.0 1.2 fusion.61
  341.2 1.2 fusion.61
  342.5 1.2 fusion.61
  343.8 1.2 fusion.61
  345.0 1.2 fusion.61
  346.3 1.2 fusion.61
  347.5 1.2 fusion.61
  348.8 1.2 fusion.61
  350.1 1.2 fusion.61
  351.3 1.2 fusion.61
  352.6 1.2 fusion.61
  353.8 158.4 %all-gather.11.cloned.1.call-done = bf16[16384,4,256]{2,0,1:T(8,128)(2,1)} async-done(((bf16[1024,4,256]{2,0,1:T(8,128)(2,1)}), bf16[16384,4,256]{2,0,1:T(8,128)(2,1)}) %all-gather.11.cloned.1.call-update) | async-done | bytes 33554448 | tf_op jit(solution)/shard_map/all_gather | solution.py:80
  512.2 34.4 %fusion.11 = bf16[4,48,64,256]{3,1,2,0:T(8,128)(2,1)S(1)} fusion(bf16[256,64,4,256]{3,1,0,2:T(8,128)(2,1)} %bitcast.65, s32[4,48]{1,0:T(4,128)S(1)} %add.84), kind=kOutput, calls=%fused_computation.20 | convolution fusion | flops 1613807616 | bytes 39846656 | tf_op jit(solution)/shard_map/hrb,bthe->hrte/dot_general | solution.py:84
  546.6 2.5 copy.42
  549.1 1.8 fusion.55
  550.9 4.1 fusion.18
  555.0 28.1 %fusion.57 = (f32[16,4,64]{2,1,0:T(4,128)S(1)}, f32[16,4,64,512]{3,2,1,0:T(8,128)}) fusion(f32[16,4,64,192]{3,2,1,0:T(8,128)} %fusion.18, f32[16,4,64,128]{3,2,1,0:T(8,128)S(1)} %convolution_bitcast_fusion, f32[16,4,64,192]{3,2,1,0:T(8,128)S(1)} %copy-done.5), kind=kOutput, calls=%fused_computation.71 | output fusion | flops 10486271 | bytes 16793600 | tf_op jit(solution)/shard_map/sub | solution.py:111
  583.1 4.1 divide_convert_fusion
  587.1 1.3 fusion.14
  588.4 1.6 fusion.36
  590.0 0.4 copy-done.3
  590.4 1.4 fusion.29
  591.8 0.1 slice.130
  591.9 0.1 copy.47
  592.0 0.1 bitcast_select_fusion
  592.1 0.1 pad_maximum_fusion.3
  592.2 1.8 copy.48
  (32 shorter events, 0.4 us)
Async XLA Ops:
  6.5 97.4 %all-gather.9.cloned.1.call-start = ((), (), s32[]{:S(2)}) async-start(), calls=%async_computation | async-start | bytes 9437184 | tf_op jit(solution)/shard_map/all_gather | solution.py:52
  7.3 254.2 %all-reduce.2.cloned.1.call-start = ((), (), s32[]{:S(2)}) async-start(), calls=%async_computation.1 | async-start | bytes 786432 | tf_op jit(solution)/shard_map/psum | solution.py:30
  122.3 144.1 %copy-start.4 = (bf16[1024,4,384]{2,0,1:T(8,128)(2,1)}, bf16[1024,4,384]{2,0,1:T(8,128)(2,1)S(1)}, u32[]{:S(2)}) copy-start(bf16[1024,4,384]{2,0,1:T(8,128)(2,1)S(1)} %fusion.22) | copy-start | bytes 9437188
  123.2 210.6 %all-gather.13.cloned.1.call-start = ((), (), s32[]{:S(2)}) async-start(), calls=%async_computation.3 | async-start | bytes 4456448 | tf_op jit(solution)/shard_map/all_gather | solution.py:34
  262.8 1.3 copy-start.1
  266.3 245.9 %all-gather.11.cloned.1.call-start = ((), (), s32[]{:S(2)}) async-start(), calls=%async_computation.2 | async-start | bytes 35651584 | tf_op jit(solution)/shard_map/all_gather | solution.py:80
  267.9 6.2 %copy-start = (bf16[1024,4,256]{2,0,1:T(8,128)(2,1)S(1)}, bf16[1024,4,256]{2,0,1:T(8,128)(2,1)}, u32[]{:S(2)}) copy-start(bf16[1024,4,256]{2,0,1:T(8,128)(2,1)} %slice.118) | copy-start | bytes 6291460
  269.7 2.9 collective-permute-start
  269.7 4.4 collective-permute-start.1
  282.8 29.6 %copy-start.2 = (f32[4,128,1024]{2,1,0:T(8,128)S(1)}, f32[4,128,1024]{2,1,0:T(8,128)}, u32[]{:S(2)}) copy-start(f32[4,128,1024]{2,1,0:T(8,128)} %copy-done.1) | copy-start | bytes 6291460
  550.9 4.1 copy-start.5
  588.4 2.0 copy-start.3
Sparse Core Ops, SparseCore 0:
  9.0 94.9 all-gather.8
  123.3 138.0 all-reduce.1
  266.4 57.4 all-gather.12
  326.3 185.8 all-gather.10
where the time goes:
time: 610 us; the launch traced here: 601 us
  waiting for transfers between devices  396 us (65%)
  matrix products  70 us (11%)
  other arithmetic  58.3 us (10%)
  blocking collectives  45 us (7%)
  local copies, waits for them, and re-layouts  17.1 us (3%)
  between operations  13.6 us (2%)
    all_gather x1, waiting for transfers between devices, per_device(): block_rows = lax.all_gather(keyval, 'ctx', axis=0, tiled=True)  158 us
    psum x1, waiting for transfers between devices, from_root(): return lax.psum(block, axis)  138 us
    all_gather x1, waiting for transfers between devices, per_device(): lax.all_gather(tokens, 'head', axis=1, tiled=True)  96.7 us
    all_gather x2, blocking collectives, combined_all(): gathered = jax.tree.map(lambda a: lax.all_gather(a, axis), part)  45 us
    dot_general x1, matrix products, per_device(): jnp.einsum('hrb,bthe->hrte', piece_hot, blocked, preferred_element_type=j...  34.4 us
    sub x1, other arithmetic, per_device(): jax.nn.softmax(logit_scores, axis=-1).astype(jnp.bfloat16)  28.1 us
    dot_general x1, matrix products, per_device(): jnp.einsum('td,dhe->the', lax.all_gather(tokens, 'head', axis=1, tiled=Tr...  18.3 us
    add x15, other arithmetic, combine(): sum_first * factor_first[..., None] + sum_second * factor_second[..., None]  18.2 us
  transfers between devices with their start and end apart: 6, of which 4 were waited for; matrix products, arithmetic and copies ran while one was open for 7% of the time, Pallas kernels for 0%

commit v1 on v0

v1 whole, which is shorter than its diff:
```python
import functools

import jax
import jax.numpy as jnp
from jax import lax
from jax.experimental import pallas as pl
from jax.experimental.pallas import tpu as pltpu
from jax.sharding import PartitionSpec as P

MESH = pl.DeviceIdType.MESH
HD = 128
BLK = 64
NB = 256
RUN = 1024
TB = 128
T = RUN // TB
LEAD = 5
GROUP = 256
GROUPS = RUN // GROUP
SCALE2 = HD**-0.5 * 1.4426950408889634


def kernel(
    x_ref, w_ref, ps_ref, pb_ref, o_ref,
    xg, wst, wv, qst, kvst, qmy, kv, gq, gm, gl, gacc, gout, grecv, ost,
    x_sem, w_sem, ag_s, ag_r, q_s, q_r, kva_s, kva_r, kvz_s, kvb_r, kvc_s, kvc_r,
    gq_s, gq_r, go_s, go_r, o_s, o_r,
):
    ctx, head = lax.axis_index("ctx"), lax.axis_index("head")
    zh, x, core = ctx // 8, (ctx // 2) % 4, ctx % 2
    zl, y = head // 4, head % 4

    def dev(zh=zh, x=x, core=core, zl=zl, y=y):
        return (zh * 8 + x * 2 + core, zl * 4 + y)

    def run_of(zh, x, core):
        return zh * 8 + x * 2 + core

    up, down = (y + 1) % 4, (y + 3) % 4
    dev_up, dev_down = dev(y=up), dev(y=down)
    dev_zl, dev_zh, dev_core = dev(zl=1 - zl), dev(zh=1 - zh), dev(core=1 - core)

    def remote(src, dst, send, recv, device):
        return pltpu.make_async_remote_copy(
            src_ref=src, dst_ref=dst, send_sem=send, recv_sem=recv,
            device_id=device, device_id_type=MESH,
        )

    own_copy = pltpu.make_async_copy(x_ref, xg.at[head], x_sem.at[0])
    own_copy.start()

    def w_copy(piece, slot):
        return pltpu.make_async_copy(
            w_ref.at[pl.ds(piece * 512, 512)], wst.at[slot], w_sem.at[slot]
        )

    w_copy(0, 0).start()
    w_copy(1, 1).start()

    barrier = pltpu.get_barrier_semaphore()
    for device in (dev_up, dev_down, dev_zl):
        pl.semaphore_signal(barrier, inc=1, device_id=device, device_id_type=MESH)
    for step in range(1, 16):
        pl.semaphore_signal(
            barrier, inc=1, device_id=((ctx + step) % 16, head), device_id_type=MESH
        )
    pl.semaphore_wait(barrier, 18)
    own_copy.wait()

    def xs_at(slot, t):
        return xg.at[slot, pl.ds(pl.multiple_of(t * TB, TB), TB)]

    def ag(kind, slot, t, device):
        return remote(xs_at(slot, t), xs_at(slot, t), ag_s.at[kind, t], ag_r.at[slot, t], device)

    other = (1 - zl) * 4

    def fwd(t):
        forward = t % 2 == 0
        own_slot = zl * 4 + jnp.where(forward, down, up)
        own_dev = jnp.where(forward, up, down)
        far_slot = other + jnp.where(forward, up, down)
        far_dev = jnp.where(forward, down, up)
        return (
            ag(5, own_slot, t, dev(y=own_dev)),
            ag(6, far_slot, t, dev(y=far_dev)),
        )

    def step1(t):
        ag(0, head, t, dev_zl).start()
        ag(1, head, t, dev_up).start()
        ag(2, head, t, dev_down).start()

    def step2(t):
        ag(0, other + y, t, dev_zl).wait_recv()
        ag(3, other + y, t, dev_up).start()
        ag(4, other + y, t, dev_down).start()

    def step3(t):
        for base in (zl * 4, other):
            for side in (up, down):
                ag(1, base + side, t, dev_up).wait_recv()
        a, b = fwd(t)
        a.start()
        b.start()

    def project(t):
        for base in (zl * 4, other):
            ag(5, base + (y + 2) % 4, t, dev_up).wait_recv()
        rows = pl.ds(pl.multiple_of(t * TB, TB), TB)
        blocks = pl.ds(t * (TB // BLK), TB // BLK)
        for n in range(6):
            acc = jnp.dot(
                xg[0, rows], wv[0:512, n * 256 : (n + 1) * 256],
                preferred_element_type=jnp.float32,
            )
            for g in range(1, 8):
                acc = acc + jnp.dot(
                    xg[g, rows], wv[g * 512 : (g + 1) * 512, n * 256 : (n + 1) * 256],
                    preferred_element_type=jnp.float32,
                )
            acc = acc.astype(jnp.bfloat16)
            if n < 2:
                qst[2 * n, rows] = acc[:, :HD]
                qst[2 * n + 1, rows] = acc[:, HD:]
            else:
                kvst[n - 2, blocks] = acc.reshape(TB // BLK, BLK, 2 * HD)

    def kv_at(zs, xs, cs, t):
        start = run_of(zs, xs, cs) * (RUN // BLK) + t * (TB // BLK)
        return kv.at[pl.ds(start, TB // BLK)]

    def q_send(j, t):
        h = (x + j) % 4
        rows = pl.ds(pl.multiple_of(t * TB, TB), TB)
        if j == 0:
            return pltpu.make_async_copy(qst.at[h, rows], qmy.at[x, rows], q_r.at[x, t])
        return remote(qst.at[h, rows], qmy.at[x, rows], q_s.at[j, t], q_r.at[x, t], dev(x=h))

    def kv_send(j, t):
        h = (x + j) % 4
        rows = pl.ds(t * (TB // BLK), TB // BLK)
        dst = kv_at(zh, x, core, t)
        if j == 0:
            return pltpu.make_async_copy(kvst.at[h, rows], dst, kva_r.at[x, t])
        return remote(kvst.at[h, rows], dst, kva_s.at[j, t], kva_r.at[x, t], dev(x=h))

    def gq_copy(target):
        h = (target // 2) % 4
        part = (target // 8) * 2 + target % 2
        src = qst.at[h, pl.ds(pl.multiple_of(part * 32, 32), 32)]
        if target == 0:
            return pltpu.make_async_copy(src, gq, gq_r.at[0])
        return remote(src, gq, gq_s.at[target], gq_r.at[0], (jnp.int32(target), head))

    def send1(t):
        for j in (2, 1, 3, 0):
            kv_send(j, t).start()
        for j in (2, 1, 3, 0):
            q_send(j, t).start()

        @pl.when((t == 0) & (ctx == 0))
        def _():
            for target in range(16):
                gq_copy(target).start()

    def z_fwd(xs, t):
        return remote(
            kv_at(zh, xs, core, t), kv_at(zh, xs, core, t),
            kvz_s.at[xs, t], kvb_r.at[xs, t], dev_zh,
        )

    def c_fwd(zs, z_slot, xs, t):
        return remote(
            kv_at(zs, xs, core, t), kv_at(zs, xs, core, t),
            kvc_s.at[z_slot * 4 + xs, t], kvc_r.at[z_slot * 4 + xs, t], dev_core,
        )

    def send2(t):
        for j in (0, 1, 3, 2):
            xs = (x + j) % 4
            rows = pl.ds(0, TB // BLK)
            pltpu.make_async_copy(kvst.at[0, rows], kv_at(zh, xs, core, t), kva_r.at[xs, t]).wait()
            z_fwd(xs, t).start()
            c_fwd(zh, 0, xs, t).start()

    def send3(t):
        for j in (0, 1, 3, 2):
            xs = (x + j) % 4
            remote(
                kv_at(zh, xs, core, t), kv_at(1 - zh, xs, core, t),
                kvz_s.at[xs, t], kvb_r.at[xs, t], dev_zh,
            ).wait_recv()
            c_fwd(1 - zh, 1, xs, t).start()

    def global_part(t):
        @pl.when(t == 0)
        def _():
            pltpu.make_async_copy(qst.at[0, pl.ds(0, 32)], gq, gq_r.at[0]).wait()
            gm[...] = jnp.full_like(gm, -1e30)
            gl[...] = jnp.zeros_like(gl)
            gacc[...] = jnp.zeros_like(gacc)

        for zslot in range(2):
            for xs in range(4):
                zs = zh if zslot == 0 else 1 - zh
                remote(
                    kv_at(zs, xs, core, t), kv_at(zs, xs, 1 - core, t),
                    kvc_s.at[zslot * 4 + xs, t], kvc_r.at[zslot * 4 + xs, t], dev_core,
                ).wait_recv()
        query = gq[...]
        for quarter in range(4):
            block = jnp.concatenate(
                [
                    kv[pl.ds((quarter * 4 + c) * (RUN // BLK) + t * (TB // BLK), TB // BLK)]
                    for c in range(4)
                ],
                axis=0,
            ).reshape(4 * TB, 2 * HD)
            s = lax.dot_general(
                query, block[:, :HD], (((1,), (1,)), ((), ())),
                preferred_element_type=jnp.float32,
            )
            old = gm[...]
            new = jnp.maximum(old, jnp.max(s, axis=1, keepdims=True))
            factor = jnp.exp2((old - new) * SCALE2)
            e = jnp.exp2((s - new[:, :1]) * SCALE2)
            gm[...] = new
            gl[...] = gl[...] * factor + jnp.sum(e, axis=1, keepdims=True)
            gacc[...] = gacc[...] * factor + jnp.dot(
                e.astype(jnp.bfloat16), block[:, HD:], preferred_element_type=jnp.float32
            )

    for t in range(LEAD):
        step1(t)

    @pl.loop(0, 4)
    def _(pair):
        for slot in range(2):
            piece = pair * 2 + slot
            w_copy(piece, slot).wait()
            for sub in range(4):
                v = jnp.swapaxes(wst[slot, sub * 128 : (sub + 1) * 128], 0, 1)
                rows = pl.ds(pl.multiple_of(piece * 512 + sub * 128, 128), 128)
                for h in range(4):
                    wv[rows, h * HD : (h + 1) * HD] = v[h][:, :HD]
                    wv[rows, 512 + h * 256 : 512 + (h + 1) * 256] = v[h][:, HD:]

            @pl.when(piece + 2 < 8)
            def _():
                w_copy(piece + 2, slot).start()

    step2(0)
    step2(1)
    step3(0)

    @pl.loop(0, T + 3)
    def _(i):
        @pl.when(i + LEAD < T)
        def _():
            step1(i + LEAD)

        @pl.when(i + 2 < T)
        def _():
            step2(i + 2)

        @pl.when(i + 1 < T)
        def _():
            step3(i + 1)

        @pl.when(i < T)
        def _():
            project(i)

        @pl.when((i >= 1) & (i - 1 < T))
        def _():
            send2(i - 1)

        @pl.when((i >= 2) & (i - 2 < T))
        def _():
            send3(i - 2)

        @pl.when(i < T)
        def _():
            send1(i)

        @pl.when(i >= 3)
        def _():
            global_part(i - 3)

    gout[...] = (gacc[...] / gl[...]).astype(jnp.bfloat16)

    def q_wait(xs, t):
        rows = pl.ds(pl.multiple_of(t * TB, TB), TB)
        pltpu.make_async_copy(qst.at[0, rows], qmy.at[xs, rows], q_r.at[xs, t]).wait()

    @pl.loop(0, T)
    def _(t):
        for xs in range(4):
            q_wait(xs, t)

    part = pl.ds(pl.multiple_of((zh * 2 + core) * 32, 32), 32)

    def go_copy():
        return remote(gout, grecv.at[x, part], go_s.at[0], go_r.at[ctx], (jnp.int32(0), head))

    def go_local():
        return pltpu.make_async_copy(gout, grecv.at[x, part], go_r.at[0])

    def o_copy(u):
        xs = (x + 3 - u // GROUPS) % 4
        piece = u % GROUPS
        rows = pl.ds(pl.multiple_of(piece * GROUP, GROUP), GROUP)
        return remote(
            ost.at[xs, rows], o_ref.at[x, rows], o_s.at[u], o_r.at[x, piece], dev(x=xs)
        )

    def o_local(u):
        piece = u % GROUPS
        rows = pl.ds(pl.multiple_of(piece * GROUP, GROUP), GROUP)
        return pltpu.make_async_copy(ost.at[x, rows], o_ref.at[x, rows], o_r.at[x, piece])

    def one_row(xs, row):
        block = run_of(zh, xs, core) * 16 + row
        q = qmy[xs, pl.ds(pl.multiple_of(row * BLK, BLK), BLK)]
        ids = [(block + NB - 1) % NB, block, (block + 1) % NB, 0, 1]
        for j in range(3):
            ids.append(ps_ref[j, x, block] * 16 + pb_ref[j, x, block])
        pairs = jnp.concatenate([kv[i] for i in ids], axis=0)
        keys, values = pairs[:, :HD], pairs[:, HD:]
        s = lax.dot_general(
            q, keys, (((1,), (1,)), ((), ())), preferred_element_type=jnp.float32
        )
        e = jnp.exp2((s - jnp.max(s, axis=1, keepdims=True)) * SCALE2)
        total = jnp.sum(e, axis=1, keepdims=True)
        out = jnp.dot(e.astype(jnp.bfloat16), values, preferred_element_type=jnp.float32)
        ost[xs, pl.ds(pl.multiple_of(row * BLK, BLK), BLK)] = (out / total).astype(jnp.bfloat16)

    @pl.loop(0, 4 * GROUPS + 1)
    def _(u):
        @pl.when(u < 4 * GROUPS)
        def _():
            xs = (x + 3 - u // GROUPS) % 4
            for k in range(GROUP // BLK):
                one_row(xs, (u % GROUPS) * (GROUP // BLK) + k)

        @pl.when((u >= 1) & (u - 1 < 3 * GROUPS))
        def _():
            o_copy(u - 1).start()

        @pl.when(u - 1 >= 3 * GROUPS)
        def _():
            o_local(u - 1).start()

        @pl.when((u == 0) & (ctx != 0))
        def _():
            go_copy().start()

        @pl.when((u == 0) & (ctx == 0))
        def _():
            go_local().start()

    for h in range(4):
        for piece in range(GROUPS):
            rows = pl.ds(piece * GROUP, GROUP)
            pltpu.make_async_copy(ost.at[0, rows], o_ref.at[h, rows], o_r.at[h, piece]).wait()

    @pl.when(ctx == 0)
    def _():
        for source in range(16):
            rows = pl.ds(((source // 8) * 2 + source % 2) * 32, 32)
            pltpu.make_async_copy(gout, grecv.at[(source // 2) % 4, rows], go_r.at[source]).wait()
        for h in range(4):
            o_ref[h, 0:128] = grecv[h]
        for target in range(1, 16):
            gq_copy(target).wait_send()

    @pl.when(ctx != 0)
    def _():
        go_copy().wait_send()

    @pl.loop(0, T)
    def _(t):
        for kind in range(3):
            ag(kind, head, t, dev_up).wait_send()
        for kind in range(3, 5):
            ag(kind, other + y, t, dev_up).wait_send()
        a, b = fwd(t)
        a.wait_send()
        b.wait_send()
        for j in range(1, 4):
            q_send(j, t).wait_send()
            kv_send(j, t).wait_send()
        for xs in range(4):
            z_fwd(xs, t).wait_send()
            c_fwd(zh, 0, xs, t).wait_send()
            c_fwd(1 - zh, 1, xs, t).wait_send()

    @pl.loop(0, 3 * GROUPS)
    def _(u):
        o_copy(u).wait_send()


def per_device(tokens, proj_weight, partner_shard, partner_block):
    bf = jnp.bfloat16
    dma = pltpu.SemaphoreType.DMA
    vmem = pl.BlockSpec(memory_space=pltpu.VMEM)
    hbm = pl.BlockSpec(memory_space=pl.ANY)
    smem = pl.BlockSpec(memory_space=pltpu.SMEM)
    out = pl.pallas_call(
        kernel,
        out_shape=jax.ShapeDtypeStruct((4, RUN, HD), bf),
        in_specs=[hbm, hbm, smem, smem],
        out_specs=vmem,
        scratch_shapes=[
            pltpu.VMEM((8, RUN, 512), bf),
            pltpu.VMEM((2, 512, 4, 384), bf),
            pltpu.VMEM((4096, 1536), bf),
            pltpu.VMEM((4, RUN, HD), bf),
            pltpu.VMEM((4, RUN // BLK, BLK, 2 * HD), bf),
            pltpu.VMEM((4, RUN, HD), bf),
            pltpu.VMEM((NB, BLK, 2 * HD), bf),
            pltpu.VMEM((32, HD), bf),
            pltpu.VMEM((32, HD), jnp.float32),
            pltpu.VMEM((32, HD), jnp.float32),
            pltpu.VMEM((32, HD), jnp.float32),
            pltpu.VMEM((32, HD), bf),
            pltpu.VMEM((4, HD, HD), bf),
            pltpu.VMEM((4, RUN, HD), bf),
            dma((1,)),
            dma((2,)),
            dma((7, T)),
            dma((8, T)),
            dma((4, T)),
            dma((4, T)),
            dma((4, T)),
            dma((4, T)),
            dma((4, T)),
            dma((4, T)),
            dma((8, T)),
            dma((8, T)),
            dma((16,)),
            dma((1,)),
            dma((1,)),
            dma((16,)),
            dma((4 * GROUPS,)),
            dma((4, GROUPS)),
        ],
        compiler_params=pltpu.CompilerParams(
            collective_id=0, has_side_effects=True, vmem_limit_bytes=60 << 20
        ),
        name="bigbird",
    )(
        tokens,
        proj_weight,
        jnp.transpose(partner_shard, (2, 0, 1)),
        jnp.transpose(partner_block, (2, 0, 1)),
    )
    return jnp.transpose(out, (1, 0, 2))


def solution(mesh):
    return jax.shard_map(
        per_device,
        mesh=mesh,
        in_specs=(P("ctx", "head"), P(None, "head", None), P("head"), P("head")),
        out_specs=P("ctx", "head", None),
        check_vma=False,
    )
```

time: 610 us -> 131 us (0.21); the launches traced: 601 us -> 131 us
  waiting for transfers between devices: 396 us -> 0 us
  Pallas kernels: 0 us -> 128 us
  matrix products: 70 us -> 0 us
  other arithmetic: 58.3 us -> 0 us
  blocking collectives: 45 us -> 0 us
  local copies, waits for them, and re-layouts: 17.1 us -> 3.01 us
  between operations: 13.6 us -> 0.01 us
    all_gather x3 -> x0, waiting for transfers between devices: 255 us -> none  [the longest x1 158 us: per_device(): block_rows = lax.all_gather(keyval, 'ctx', axis=0, tiled=True)]
    psum x1 -> x0, waiting for transfers between devices: 138 us -> none  [from_root(): return lax.psum(block, axis)]
    pallas_call x0 -> x1, Pallas kernels: none -> 128 us  [per_device(): pl.pallas_call(kernel, out_shape=jax.ShapeDtypeStruct((4, RUN, HD), bf),...]
    dot_general x10 -> x0, matrix products: 70 us -> none  [the longest x1 34.4 us: per_device(): jnp.einsum('hrb,bthe->hrte', piece_hot, blocked, preferred_element_type=j...]
    all_gather x2 -> x0, blocking collectives: 45 us -> none  [combined_all(): gathered = jax.tree.map(lambda a: lax.all_gather(a, axis), part)]
    sub x1 -> x0, other arithmetic: 28.1 us -> none  [per_device(): jax.nn.softmax(logit_scores, axis=-1).astype(jnp.bfloat16)]
    add x31 -> x0, other arithmetic: 19.4 us -> none  [the longest x15 18.2 us: combine(): sum_first * factor_first[..., None] + sum_second * factor_second[..., None]]
    slice x9 -> x0, local copies, waits for them, and re-layouts: 10 us -> none  [the longest x1 3.45 us: per_device(): window[..., HEAD_DIMENSION:]]
  transfers between devices with their start and end apart: 6 -> 0, of which waited for: 4 -> 0; matrix products, arithmetic and copies ran while one was open for 7% -> 0% of each run, Pallas kernels for 0% -> 0%
where the time goes in v1:
time: 131 us
  Pallas kernels  128 us (98%)
  local copies, waits for them, and re-layouts  3.01 us (2%)
    pallas_call x1, Pallas kernels, per_device(): pl.pallas_call(kernel, out_shape=jax.ShapeDtypeStruct((4, RUN, HD), bf),...  128 us
    transpose x1, local copies, waits for them, and re-layouts, per_device(): return jnp.transpose(out, (1, 0, 2))  3.01 us

profile of v1, /device:TPU:1, one launch (start us, length us, event | category | flops | bytes accessed | tf_op | source)
XLA Modules:
  0.0 130.7 jit_solution(14340899819051815662)
XLA Ops:
  0.0 127.7 %bigbird.1 = bf16[4,1024,128]{2,1,0:T(8,128)(2,1)} custom-call(bf16[1024,512]{1,0:T(8,128)(2,1)} %x_ref.1, bf16[4096,4,384]{2,1,0:T(4,128)(2,1)} %w_ref.1, s32[3,4,256]{2,1,0:T(4,128)} %bitcast.4, s32[3,4,256]{2,1,0:T(4,128)} %bitcast.5), custom_call_target="tpu_custom_call" | custom-call | tf_op jit(solution)/shard_map/bigbird/pallas_call | solution.py:410
  127.7 3.0 %copy.5 = bf16[1024,4,128]{2,1,0:T(4,128)(2,1)} copy(bf16[1024,4,128]{2,0,1:T(8,128)(2,1)} %bitcast.3) | data formatting | bytes 2097152 | tf_op jit(solution)/shard_map/transpose | solution.py:459
